TPU v7x, 128 devices: a whole 4x4x4 slice. The times are simulated.
128 devices in a mesh: row: 8 (over y, core), col: 16 (over z, x).
Axes of the slice: x: 4, y: 4, z: 4, core: 2. Of those that a mesh axis runs over, the one named last changes fastest.
Arguments:
- points: float32 [3, 262144], P(None, ('row', 'col')), as said below
- values: float32 [16, 262144], P(None, ('row', 'col'))
- tile_lists: int32 [3, 6144], P(None, ('row', 'col')), may hold values from 0 to 127, as said below
Outputs:
- solution: float32 [16, 262144], P(None, ('row', 'col'))
- residual: float32 [16, 262144], P(None, ('row', 'col'))
Inputs may be any that keep to these rules, and one draw needn't show every extreme that they name: `tile_lists`: on every device the live slots come first and the rest hold 0, 0, 0; a device holds at most 48 live slots and some device holds exactly that many; no unordered pair of blocks is listed twice, in either order. Block pairs whose points can come within the support radius are listed. Coordinates of point blocks that lie in cells of a square lattice of unit cells, 256 points to a block.
All inputs are finite; a program needn't handle non-finite values.
Results may differ from a plain program's by a relative error of at most 0.0003.
Values sent between devices are 32-bit elements; how exact they have to be, the bound alone decides.
A program may use at most 64 MiB of HBM per device.

v0:
```python
import jax
import jax.numpy as jnp
from jax import lax
from jax.sharding import PartitionSpec as P

BLK = 256
ITERS = 2
support = 0.5
ridge_shift = 1.0
group_width = 12


def wendland(left, right):
    offsets = left[:, :, :, None] - right[:, :, None, :]
    distance = jnp.sqrt(jnp.sum(offsets * offsets, axis=0))
    scaled = distance / support
    remain = jnp.maximum(1.0 - scaled, 0.0)
    return remain * remain * remain * remain * (4.0 * scaled + 1.0)


def local(points, values, tile_lists):
    fields, owned_points = values.shape
    per_device = owned_points // BLK
    col_count = lax.axis_size("col")
    row_count = lax.axis_size("row")
    row_id = lax.axis_index("row")
    col_id = lax.axis_index("col")
    row_span = col_count * per_device
    col_span = row_count * per_device
    cloud_rows = lax.all_gather(points, "col", axis=1, tiled=True).reshape(3, row_span, BLK)
    cloud_cols = lax.all_gather(points, "row", axis=1, tiled=True).reshape(3, col_span, BLK)
    row_local = tile_lists[0]
    col_local = tile_lists[1]
    row_block = row_id * row_span + row_local
    col_block = (col_local // per_device * col_count + col_id) * per_device + col_local % per_device
    weight = tile_lists[2].astype(jnp.float32)
    mirror_weight = weight * (row_block != col_block).astype(jnp.float32)
    group_count = tile_lists.shape[1] // group_width
    group_shape = (group_count, group_width)
    groups = (
        row_local.reshape(group_shape),
        col_local.reshape(group_shape),
        weight.reshape(group_shape),
        mirror_weight.reshape(group_shape),
    )

    def accumulate(totals, member_set, along_rows, along_cols):
        forward_total, behind_total = totals
        row_index, col_index, row_weight, col_weight = member_set
        kernel = wendland(cloud_rows[:, row_index], cloud_cols[:, col_index])
        forward = jnp.einsum(
            "gxy,fgy->fgx", kernel, along_cols[:, col_index], precision=lax.Precision.HIGHEST
        )
        behind = jnp.einsum(
            "gxy,fgx->fgy", kernel, along_rows[:, row_index], precision=lax.Precision.HIGHEST
        )
        forward_total = forward_total.at[:, row_index].add(forward * row_weight[None, :, None])
        behind_total = behind_total.at[:, col_index].add(behind * col_weight[None, :, None])
        return (forward_total, behind_total)

    def squares(vector):
        return lax.psum(jnp.sum(vector * vector, axis=1), ("row", "col"))

    solution = jnp.zeros_like(values)
    residual = values
    direction = values
    norm_now = squares(residual)
    for iteration in range(ITERS):
        operate_along_rows = lax.all_gather(direction, "col", axis=1, tiled=True).reshape(
            fields, row_span, BLK
        )
        operate_along_cols = lax.all_gather(direction, "row", axis=1, tiled=True).reshape(
            fields, col_span, BLK
        )
        initial = (
            jnp.zeros((fields, row_span, BLK), jnp.float32),
            jnp.zeros((fields, col_span, BLK), jnp.float32),
        )

        def visit_all(totals, member_set):
            return (accumulate(totals, member_set, operate_along_rows, operate_along_cols), None)

        (operate_forward_total, operate_behind_total), _ = lax.scan(visit_all, initial, groups)
        mine_forward = lax.psum_scatter(
            operate_forward_total.reshape(fields, row_span * BLK),
            "col",
            scatter_dimension=1,
            tiled=True,
        )
        mine_behind = lax.psum_scatter(
            operate_behind_total.reshape(fields, col_span * BLK),
            "row",
            scatter_dimension=1,
            tiled=True,
        )
        applied = ridge_shift * direction + mine_forward + mine_behind
        curve_sum = lax.psum(jnp.sum(direction * applied, axis=1), ("row", "col"))
        step_length = norm_now / curve_sum
        solution = solution + step_length[:, None] * direction
        residual = residual - step_length[:, None] * applied
        norm_next = squares(residual)
        direction = residual + (norm_next / norm_now)[:, None] * direction
        norm_now = norm_next
    return (solution, residual)


def solution(mesh):
    placed = (P(None, ("row", "col")), P(None, ("row", "col")), P(None, ("row", "col")))
    return jax.shard_map(
        local,
        mesh=mesh,
        in_specs=placed,
        out_specs=(P(None, ("row", "col")), P(None, ("row", "col"))),
        check_vma=False,
    )
```

profile of v0, /device:TPU:1, one launch (start us, length us, event | category | flops | bytes accessed | tf_op | source)
XLA Modules:
  0.0 775.9 jit_solution(17273977491042123347)
XLA Ops:
  11.6 16.0 %all_gather.20 = f32[3,16384]{1,0:T(4,128)} all-gather(f32[3,2048]{1,0:T(4,128)} %param.7), channel_id=1, replica_groups=mesh['row'=8,'col'=16] {'row'}, dimensions={1}, use_global_device_ids=true | all-gather | bytes 221184 | tf_op jit(solution)/shard_map/all_gather | solution.py:31
  27.5 23.3 %all_gather.19 = f32[3,32768]{1,0:T(4,128)} all-gather(f32[3,2048]{1,0:T(4,128)} %param.7), channel_id=1, replica_groups=mesh['row'=8,'col'=16] {'col'}, dimensions={1}, use_global_device_ids=true | all-gather | bytes 417792 | tf_op jit(solution)/shard_map/all_gather | solution.py:30
  54.5 27.5 %all-gather.7.cloned.1.call-done = f32[16,32768]{1,0:T(8,128)} async-done(((f32[16,2048]{1,0:T(8,128)}), f32[16,32768]{1,0:T(8,128)}) %all-gather.7.cloned.1.call-update) | async-done | bytes 2097168 | tf_op jit(solution)/shard_map/all_gather | solution.py:69
  82.0 3.3 copy.60
  85.6 96.3 %while.28 = (s32[]{:T(128)}, f32[16,128,256]{2,0,1:T(8,128)S(1)}, f32[16,64,256]{2,0,1:T(8,128)S(1)}, s32[4,12]{1,0:T(4,128)}, s32[4,12]{1,0:T(4,128)S(1)}, /*in...) while((s32[]{:T(128)}, f32[16,128,256]{2,0,1:T(8,128)S(1)}, ...), condition=%wide.region_6.7_spmd, body=%wide.region_2.6_spmd.sunk | while | flops 322635840 | bytes 12567965 | solution.py:83
  98.8 3.9 fusion.85
  102.7 4.1 fusion.84
  122.9 3.9 fusion.85
  126.8 4.1 fusion.84
  146.9 3.9 fusion.85
  150.8 4.1 fusion.84
  171.0 3.9 fusion.85
  174.9 4.1 fusion.84
  184.7 28.9 %reduce-scatter.7.cloned.1.call-done = f32[16,2048]{1,0:T(8,128)} async-done(((f32[16,16384]{1,0:T(8,128)}), f32[16,2048]{1,0:T(8,128)}) %reduce-scatter.7.cloned.1.call-update) | async-done | bytes 131088 | tf_op jit(solution)/shard_map/reduce_scatter | solution.py:90
  213.6 78.3 %reduce-scatter.5.cloned.1.call-done = f32[16,2048]{1,0:T(8,128)} async-done(((f32[16,32768]{1,0:T(8,128)}), f32[16,2048]{1,0:T(8,128)}) %reduce-scatter.5.cloned.1.call-update) | async-done | bytes 131088 | tf_op jit(solution)/shard_map/reduce_scatter | solution.py:84
  293.1 66.1 %all-reduce = (f32[16]{0:T(128)S(1)}, f32[16]{0:T(128)S(1)}) all-reduce(f32[16]{0:T(128)S(1)} %get-tuple-element.338, f32[16]{0:T(128)S(1)} %get-tuple-element.337), channel_id=1, replica_groups=mesh['row'=8,'col'=16] {'row','col'}, use_global_device_ids=true, to_apply=%region_1.2 | all-reduce | flops 32 | bytes 256 | tf_op jit(solution)/shard_map/psum | solution.py:62
  360.3 62.5 %psum.30 = f32[16]{0:T(128)S(1)} all-reduce(f32[16]{0:T(128)S(1)} %get-tuple-element.387), channel_id=1, replica_groups=mesh['row'=8,'col'=16] {'row','col'}, use_global_device_ids=true, to_apply=%region_12.13 | all-reduce | flops 16 | bytes 128 | tf_op jit(solution)/shard_map/psum | solution.py:62
  424.2 20.3 %all-gather.9.cloned.1.call-done = f32[16,16384]{1,0:T(8,128)} async-done(((f32[16,2048]{1,0:T(8,128)}), f32[16,16384]{1,0:T(8,128)}) %all-gather.9.cloned.1.call-update) | async-done | bytes 1048592 | tf_op jit(solution)/shard_map/all_gather | solution.py:72
  446.8 43.3 %all-gather.11.cloned.1.call-done = f32[16,32768]{1,0:T(8,128)} async-done(((f32[16,2048]{1,0:T(8,128)}), f32[16,32768]{1,0:T(8,128)}) %all-gather.11.cloned.1.call-update) | async-done | bytes 2097168 | tf_op jit(solution)/shard_map/all_gather | solution.py:69
  490.2 3.3 copy.59
  493.8 96.3 %while.29 = (s32[]{:T(128)}, f32[16,128,256]{2,0,1:T(8,128)S(1)}, f32[16,64,256]{2,0,1:T(8,128)S(1)}, s32[4,12]{1,0:T(4,128)}, s32[4,12]{1,0:T(4,128)S(1)}, /*in...) while((s32[]{:T(128)}, f32[16,128,256]{2,0,1:T(8,128)S(1)}, ...), condition=%wide.region_17.18_spmd, body=%wide.region_13.17_spmd.sunk | while | flops 322635840 | bytes 12567965 | solution.py:83
  507.0 3.9 fusion.93
  510.9 4.1 fusion.92
  531.0 3.9 fusion.93
  534.9 4.1 fusion.92
  555.1 3.9 fusion.93
  559.0 4.1 fusion.92
  579.2 3.9 fusion.93
  583.1 4.1 fusion.92
  592.9 28.9 %reduce-scatter.11.cloned.1.call-done = f32[16,2048]{1,0:T(8,128)} async-done(((f32[16,16384]{1,0:T(8,128)}), f32[16,2048]{1,0:T(8,128)}) %reduce-scatter.11.cloned.1.call-update) | async-done | bytes 131088 | tf_op jit(solution)/shard_map/reduce_scatter | solution.py:90
  621.8 78.5 %reduce-scatter.9.cloned.1.call-done = f32[16,2048]{1,0:T(8,128)} async-done(((f32[16,32768]{1,0:T(8,128)}), f32[16,2048]{1,0:T(8,128)}) %reduce-scatter.9.cloned.1.call-update) | async-done | bytes 131088 | tf_op jit(solution)/shard_map/reduce_scatter | solution.py:84
  701.3 65.9 %psum.31 = f32[16]{0:T(128)S(1)} all-reduce(f32[16]{0:T(128)S(1)} %multiply_reduce_fusion.2), channel_id=1, replica_groups=mesh['row'=8,'col'=16] {'row','col'}, use_global_device_ids=true, to_apply=%region_21.22 | all-reduce | flops 16 | bytes 128 | tf_op jit(solution)/shard_map/psum | solution.py:97
  (195 shorter events, 151.3 us)
Async XLA Ops:
  7.2 45.0 %all-gather.5.cloned.1.call-start = ((), (), s32[]{:S(2)}) async-start(), calls=%async_computation.4 | async-start | bytes 1179648 | tf_op jit(solution)/shard_map/all_gather | solution.py:72
  7.9 74.1 %all-gather.7.cloned.1.call-start = ((), (), s32[]{:S(2)}) async-start(), calls=%async_computation.5 | async-start | bytes 2228224 | tf_op jit(solution)/shard_map/all_gather | solution.py:69
  8.6 205.0 %reduce-scatter.7.cloned.1.call-start = ((), (), s32[]{:S(2)}) async-start(), calls=%async_computation.7 | async-start | bytes 1179648 | tf_op jit(solution)/shard_map/reduce_scatter | solution.py:90
  96.0 2.8 copy-start.7
  98.8 3.9 copy-start.5
  120.1 2.8 copy-start.7
  122.9 3.9 copy-start.5
  144.1 2.8 copy-start.7
  146.9 3.9 copy-start.5
  168.2 2.8 copy-start.7
  171.0 3.9 copy-start.5
  183.1 108.9 %reduce-scatter.5.cloned.1.call-start = ((), (), s32[]{:S(2)}) async-start(), calls=%async_computation.6 | async-start | bytes 2228224 | tf_op jit(solution)/shard_map/reduce_scatter | solution.py:84
  183.1 108.8 %copy-start = (f32[16,2048]{1,0:T(8,128)S(1)}, f32[16,2048]{1,0:T(8,128)}, u32[]{:S(2)}) copy-start(f32[16,2048]{1,0:T(8,128)} %param.8) | copy-start | bytes 393220
  184.7 259.8 %all-gather.9.cloned.1.call-start = ((), (), s32[]{:S(2)}) async-start(), calls=%async_computation.8 | async-start | bytes 1179648 | tf_op jit(solution)/shard_map/all_gather | solution.py:72
  359.2 134.3 %copy-start.9 = (f32[16]{0:T(128)}, f32[16]{0:T(128)S(1)}, u32[]{:S(2)}) copy-start(f32[16]{0:T(128)S(1)} %div.31) | copy-start | bytes 196
  360.3 133.1 %copy-start.3 = (f32[16,2048]{1,0:T(8,128)}, f32[16,2048]{1,0:T(8,128)S(1)}, u32[]{:S(2)}) copy-start(f32[16,2048]{1,0:T(8,128)S(1)} %get-tuple-element.388) | copy-start | bytes 393220
  422.8 70.6 %copy-start.11 = (f32[16]{0:T(128)}, f32[16]{0:T(128)S(1)}, u32[]{:S(2)}) copy-start(f32[16]{0:T(128)S(1)} %psum.30) | copy-start | bytes 196
  423.6 66.5 %all-gather.11.cloned.1.call-start = ((), (), s32[]{:S(2)}) async-start(), calls=%async_computation.9 | async-start | bytes 2228224 | tf_op jit(solution)/shard_map/all_gather | solution.py:69
  424.2 197.6 %reduce-scatter.11.cloned.1.call-start = ((), (), s32[]{:S(2)}) async-start(), calls=%async_computation.11 | async-start | bytes 1179648 | tf_op jit(solution)/shard_map/reduce_scatter | solution.py:90
  504.1 2.8 copy-start.8
  507.0 3.9 copy-start.6
  528.2 2.8 copy-start.8
  531.0 3.9 copy-start.6
  552.3 2.8 copy-start.8
  555.1 3.9 copy-start.6
  579.2 3.9 copy-start.6
  591.2 109.0 %reduce-scatter.9.cloned.1.call-start = ((), (), s32[]{:S(2)}) async-start(), calls=%async_computation.10 | async-start | bytes 2228224 | tf_op jit(solution)/shard_map/reduce_scatter | solution.py:84
  591.3 109.0 %copy-start.2 = (f32[16,2048]{1,0:T(8,128)S(1)}, f32[16,2048]{1,0:T(8,128)}, u32[]{:S(2)}) copy-start(f32[16,2048]{1,0:T(8,128)} %multiply_add_fusion.1) | copy-start | bytes 393220
  591.3 176.0 %copy-start.12 = (f32[16]{0:T(128)S(1)}, f32[16]{0:T(128)}, u32[]{:S(2)}) copy-start(f32[16]{0:T(128)} %copy-done.11) | copy-start | bytes 196
  591.3 176.0 %copy-start.1 = (f32[16,2048]{1,0:T(8,128)S(1)}, f32[16,2048]{1,0:T(8,128)}, u32[]{:S(2)}) copy-start(f32[16,2048]{1,0:T(8,128)} %param.8) | copy-start | bytes 393220
  591.3 176.0 %copy-start.4 = (f32[16,2048]{1,0:T(8,128)S(1)}, f32[16,2048]{1,0:T(8,128)}, u32[]{:S(2)}) copy-start(f32[16,2048]{1,0:T(8,128)} %copy-done.3) | copy-start | bytes 393220
  591.3 176.0 %copy-start.10 = (f32[16]{0:T(128)S(1)}, f32[16]{0:T(128)}, u32[]{:S(2)}) copy-start(f32[16]{0:T(128)} %copy-done.9) | copy-start | bytes 196
  (1 other events, 2.8 us)
Sparse Core Ops, SparseCore 0:
  9.7 26.8 all-gather.4
  38.7 43.2 all-gather.6
  183.2 30.3 reduce-scatter.6
  216.8 75.1 reduce-scatter.4
  423.7 20.7 all-gather.8
  447.1 43.0 all-gather.10
  591.3 30.3 reduce-scatter.10
  625.0 75.1 reduce-scatter.8
where the time goes:
time: 779 us; the launch traced here: 776 us
  waiting for transfers between devices  308 us (40%)
  blocking collectives  234 us (30%)
  local copies, waits for them, and re-layouts  96.2 us (12%)
  matrix products  63.5 us (8%)
  other arithmetic  59.3 us (8%)
  between operations  14.3 us (2%)
    reduce_scatter x2, waiting for transfers between devices, local(): lax.psum_scatter(operate_forward_total.reshape(fields, row_span * BLK), '...  157 us
    psum x2, blocking collectives, squares(): return lax.psum(jnp.sum(vector * vector, axis=1), ('row', 'col'))  129 us
    all_gather x2, waiting for transfers between devices, local(): lax.all_gather(direction, 'col', axis=1, tiled=True)  70.8 us
    psum x1, blocking collectives, local(): curve_sum = lax.psum(jnp.sum(direction * applied, axis=1), ('row', 'col'))  65.9 us
    reduce_scatter x2, waiting for transfers between devices, local(): lax.psum_scatter(operate_behind_total.reshape(fields, col_span * BLK), 'r...  57.8 us
    gather x32, local copies, waits for them, and re-layouts, accumulate(): kernel = wendland(cloud_rows[:, row_index], cloud_cols[:, col_index])  35.2 us
    dot_general x8, matrix products, accumulate(): jnp.einsum('gxy,fgy->fgx', kernel, along_cols[:, col_index], precision=la...  32.4 us
    dot_general x8, matrix products, accumulate(): jnp.einsum('gxy,fgx->fgy', kernel, along_rows[:, row_index], precision=la...  31.1 us
  transfers between devices with their start and end apart: 8, of which 7 were waited for; matrix products, arithmetic and copies ran while one was open for 2% of the time, Pallas kernels for 0%

commit v1 on v0

--- a/solution.py
+++ b/solution.py
@@ -8,6 +8,12 @@
 support = 0.5
 ridge_shift = 1.0
 group_width = 12
+
+
+def _make_results(arr_in):
+    return jnp.concatenate(
+        lax.all_to_all(jnp.stack(lax.axis_size("col") * [arr_in], axis=0), "col", 0, 0), axis=1
+    )
 
 
 def wendland(left, right):
@@ -66,9 +72,7 @@
     direction = values
     norm_now = squares(residual)
     for iteration in range(ITERS):
-        operate_along_rows = lax.all_gather(direction, "col", axis=1, tiled=True).reshape(
-            fields, row_span, BLK
-        )
+        operate_along_rows = _make_results(direction).reshape(fields, row_span, BLK)
         operate_along_cols = lax.all_gather(direction, "row", axis=1, tiled=True).reshape(
             fields, col_span, BLK
         )

time: 779 us -> 740 us (0.950)
  waiting for transfers between devices: 308 us -> 244 us
  starting transfers between devices: 0.32 us -> 13 us
  local copies, waits for them, and re-layouts: 96.2 us -> 107 us
    all_gather x2 -> x0, waiting for transfers between devices: 70.8 us -> none  [local(): lax.all_gather(direction, 'col', axis=1, tiled=True)]
    all_to_all x0 -> x2, starting transfers between devices: none -> 12.8 us  [_make_results(): lax.all_to_all(jnp.stack(lax.axis_size('col') * [arr_in], axis=0), 'col',...]
  transfers between devices with their start and end apart: 8 -> 8, of which waited for: 7 -> 6; matrix products, arithmetic and copies ran while one was open for 2% -> 1% of each run, Pallas kernels for 0% -> 0%
where the time goes in v1:
time: 740 us; the launch traced here: 737 us
  waiting for transfers between devices  244 us (33%)
  blocking collectives  236 us (32%)
  local copies, waits for them, and re-layouts  107 us (14%)
  matrix products  63.5 us (9%)
  other arithmetic  57.9 us (8%)
  between operations  14.3 us (2%)
  starting transfers between devices  13 us (2%)
    reduce_scatter x2, waiting for transfers between devices, local(): lax.psum_scatter(operate_forward_total.reshape(fields, row_span * BLK), '...  157 us
    psum x2, blocking collectives, squares(): return lax.psum(jnp.sum(vector * vector, axis=1), ('row', 'col'))  129 us
    psum x1, blocking collectives, local(): curve_sum = lax.psum(jnp.sum(direction * applied, axis=1), ('row', 'col'))  65.9 us
    reduce_scatter x2, waiting for transfers between devices, local(): lax.psum_scatter(operate_behind_total.reshape(fields, col_span * BLK), 'r...  58.3 us
    gather x32, local copies, waits for them, and re-layouts, accumulate(): kernel = wendland(cloud_rows[:, row_index], cloud_cols[:, col_index])  35.2 us
    dot_general x8, matrix products, accumulate(): jnp.einsum('gxy,fgy->fgx', kernel, along_cols[:, col_index], precision=la...  32.4 us
    dot_general x8, matrix products, accumulate(): jnp.einsum('gxy,fgx->fgy', kernel, along_rows[:, row_index], precision=la...  31.1 us
    all_gather x2, waiting for transfers between devices, local(): lax.all_gather(direction, 'row', axis=1, tiled=True)  26.2 us
  transfers between devices with their start and end apart: 8, of which 6 were waited for; matrix products, arithmetic and copies ran while one was open for 1% of the time, Pallas kernels for 0%

profile of v1, /device:TPU:1, one launch (start us, length us, event | category | flops | bytes accessed | tf_op | source)
XLA Modules:
  0.0 736.8 jit_solution(7644636011493723863)
XLA Ops:
  9.7 8.4 %all-to-all-start = ((f32[16,16,2048]{2,1,0:T(8,128)}), f32[16,16,2048]{2,1,0:T(8,128)S(1)}, u32[]{:S(2)}, u32[]{:S(2)}) async-start(f32[16,16,2048]{2,1,0:T(8,128)} %stack.4), calls=%async_computation | async-start | bytes 4194304 | tf_op jit(solution)/shard_map/all_to_all | solution.py:15
  20.4 15.2 %all_gather.14 = f32[3,16384]{1,0:T(4,128)} all-gather(f32[3,2048]{1,0:T(4,128)S(1)} %copy-done.6), channel_id=1, replica_groups=mesh['row'=8,'col'=16] {'row'}, dimensions={1}, use_global_device_ids=true | all-gather | bytes 221184 | tf_op jit(solution)/shard_map/all_gather | solution.py:37
  35.6 25.8 %all_gather.13 = f32[3,32768]{1,0:T(4,128)} all-gather(f32[3,2048]{1,0:T(4,128)S(1)} %copy-done.6), channel_id=1, replica_groups=mesh['row'=8,'col'=16] {'col'}, dimensions={1}, use_global_device_ids=true | all-gather | bytes 417792 | tf_op jit(solution)/shard_map/all_gather | solution.py:36
  72.3 96.3 %while.28 = (s32[]{:T(128)}, f32[16,128,256]{2,0,1:T(8,128)S(1)}, f32[16,64,256]{2,0,1:T(8,128)S(1)}, s32[4,12]{1,0:T(4,128)}, s32[4,12]{1,0:T(4,128)S(1)}, /*in...) while((s32[]{:T(128)}, f32[16,128,256]{2,0,1:T(8,128)S(1)}, ...), condition=%wide.region_6.7_spmd, body=%wide.region_2.6_spmd.sunk | while | flops 322635840 | bytes 12567965 | solution.py:87
  85.5 3.9 fusion.85
  89.4 4.1 fusion.84
  109.5 3.9 fusion.85
  113.4 4.1 fusion.84
  133.6 3.9 fusion.85
  137.5 4.1 fusion.84
  157.7 3.9 fusion.85
  161.6 4.1 fusion.84
  171.3 32.6 %reduce-scatter.7.cloned.1.call-done = f32[16,2048]{1,0:T(8,128)} async-done(((f32[16,16384]{1,0:T(8,128)}), f32[16,2048]{1,0:T(8,128)}) %reduce-scatter.7.cloned.1.call-update) | async-done | bytes 131088 | tf_op jit(solution)/shard_map/reduce_scatter | solution.py:94
  203.9 78.4 %reduce-scatter.5.cloned.1.call-done = f32[16,2048]{1,0:T(8,128)} async-done(((f32[16,32768]{1,0:T(8,128)}), f32[16,2048]{1,0:T(8,128)}) %reduce-scatter.5.cloned.1.call-update) | async-done | bytes 131088 | tf_op jit(solution)/shard_map/reduce_scatter | solution.py:88
  283.5 66.1 %all-reduce = (f32[16]{0:T(128)S(1)}, f32[16]{0:T(128)S(1)}) all-reduce(f32[16]{0:T(128)S(1)} %get-tuple-element.360, f32[16]{0:T(128)S(1)} %get-tuple-element.359), channel_id=1, replica_groups=mesh['row'=8,'col'=16] {'row','col'}, use_global_device_ids=true, to_apply=%region_1.2 | all-reduce | flops 32 | bytes 256 | tf_op jit(solution)/shard_map/psum | solution.py:68
  350.7 62.5 %psum.30 = f32[16]{0:T(128)S(1)} all-reduce(f32[16]{0:T(128)S(1)} %get-tuple-element.409), channel_id=1, replica_groups=mesh['row'=8,'col'=16] {'row','col'}, use_global_device_ids=true, to_apply=%region_12.13 | all-reduce | flops 16 | bytes 128 | tf_op jit(solution)/shard_map/psum | solution.py:68
  415.4 4.4 all-to-all-start.1
  420.4 26.2 %all-gather.5.cloned.1.call-done = f32[16,16384]{1,0:T(8,128)} async-done(((f32[16,2048]{1,0:T(8,128)}), f32[16,16384]{1,0:T(8,128)}) %all-gather.5.cloned.1.call-update) | async-done | bytes 1048592 | tf_op jit(solution)/shard_map/all_gather | solution.py:76
  458.1 96.3 %while.29 = (s32[]{:T(128)}, f32[16,128,256]{2,0,1:T(8,128)S(1)}, f32[16,64,256]{2,0,1:T(8,128)S(1)}, s32[4,12]{1,0:T(4,128)}, s32[4,12]{1,0:T(4,128)S(1)}, /*in...) while((s32[]{:T(128)}, f32[16,128,256]{2,0,1:T(8,128)S(1)}, ...), condition=%wide.region_17.18_spmd, body=%wide.region_13.17_spmd.sunk | while | flops 322635840 | bytes 12567965 | solution.py:87
  468.5 2.8 multiply_reduce_fusion.9
  471.3 3.9 fusion.93
  475.2 4.1 fusion.92
  495.3 3.9 fusion.93
  499.2 4.1 fusion.92
  519.4 3.9 fusion.93
  523.3 4.1 fusion.92
  540.7 2.8 multiply_reduce_fusion.9
  543.5 3.9 fusion.93
  547.4 4.1 fusion.92
  557.2 25.7 %reduce-scatter.11.cloned.1.call-done = f32[16,2048]{1,0:T(8,128)} async-done(((f32[16,16384]{1,0:T(8,128)}), f32[16,2048]{1,0:T(8,128)}) %reduce-scatter.11.cloned.1.call-update) | async-done | bytes 131088 | tf_op jit(solution)/shard_map/reduce_scatter | solution.py:94
  582.9 78.3 %reduce-scatter.9.cloned.1.call-done = f32[16,2048]{1,0:T(8,128)} async-done(((f32[16,32768]{1,0:T(8,128)}), f32[16,2048]{1,0:T(8,128)}) %reduce-scatter.9.cloned.1.call-update) | async-done | bytes 131088 | tf_op jit(solution)/shard_map/reduce_scatter | solution.py:88
  662.3 65.9 %psum.31 = f32[16]{0:T(128)S(1)} all-reduce(f32[16]{0:T(128)S(1)} %multiply_reduce_fusion.2), channel_id=1, replica_groups=mesh['row'=8,'col'=16] {'row','col'}, use_global_device_ids=true, to_apply=%region_21.22 | all-reduce | flops 16 | bytes 128 | tf_op jit(solution)/shard_map/psum | solution.py:101
  (205 shorter events, 163.1 us)
Async XLA Ops:
  7.2 11.7 %copy-start.13 = (s32[3,48]{1,0:T(4,128)S(1)}, s32[3,48]{1,0:T(4,128)}, u32[]{:S(2)}) copy-start(s32[3,48]{1,0:T(4,128)} %param.9) | copy-start | bytes 1732
  7.2 13.2 %copy-start.6 = (f32[3,2048]{1,0:T(4,128)S(1)}, f32[3,2048]{1,0:T(4,128)}, u32[]{:S(2)}) copy-start(f32[3,2048]{1,0:T(4,128)} %param.7) | copy-start | bytes 73732
  9.7 55.4 %all-to-all-start = ((f32[16,16,2048]{2,1,0:T(8,128)}), f32[16,16,2048]{2,1,0:T(8,128)S(1)}, u32[]{:S(2)}, u32[]{:S(2)}) async-start(f32[16,16,2048]{2,1,0:T(8,128)} %stack.4), calls=%async_computation | async-start | bytes 4194304 | tf_op jit(solution)/shard_map/all_to_all | solution.py:15
  18.1 44.6 %all-gather.3.cloned.1.call-start = ((), (), s32[]{:S(2)}) async-start(), calls=%async_computation.6 | async-start | bytes 1179648 | tf_op jit(solution)/shard_map/all_gather | solution.py:76
  18.8 185.1 %reduce-scatter.7.cloned.1.call-start = ((), (), s32[]{:S(2)}) async-start(), calls=%async_computation.8 | async-start | bytes 1179648 | tf_op jit(solution)/shard_map/reduce_scatter | solution.py:94
  82.6 2.8 copy-start.9
  85.5 3.9 copy-start.7
  106.7 2.8 copy-start.9
  109.5 3.9 copy-start.7
  130.8 2.8 copy-start.9
  133.6 3.9 copy-start.7
  154.9 2.8 copy-start.9
  157.7 3.9 copy-start.7
  169.7 112.6 %reduce-scatter.5.cloned.1.call-start = ((), (), s32[]{:S(2)}) async-start(), calls=%async_computation.7 | async-start | bytes 2228224 | tf_op jit(solution)/shard_map/reduce_scatter | solution.py:88
  169.8 112.6 %copy-start = (f32[16,2048]{1,0:T(8,128)S(1)}, f32[16,2048]{1,0:T(8,128)}, u32[]{:S(2)}) copy-start(f32[16,2048]{1,0:T(8,128)} %param.8) | copy-start | bytes 393220
  349.6 63.7 %copy-start.11 = (f32[16]{0:T(128)}, f32[16]{0:T(128)S(1)}, u32[]{:S(2)}) copy-start(f32[16]{0:T(128)S(1)} %div.31) | copy-start | bytes 196
  350.7 64.7 %copy-start.4 = (f32[16,2048]{1,0:T(8,128)}, f32[16,2048]{1,0:T(8,128)S(1)}, u32[]{:S(2)}) copy-start(f32[16,2048]{1,0:T(8,128)S(1)} %get-tuple-element.410) | copy-start | bytes 393220
  415.4 35.5 %all-to-all-start.1 = ((f32[16,16,2048]{2,1,0:T(8,128)}), f32[16,16,2048]{2,1,0:T(8,128)S(1)}, u32[]{:S(2)}, u32[]{:S(2)}) async-start(f32[16,16,2048]{2,1,0:T(8,128)} %stack.5), calls=%async_computation.3 | async-start | bytes 4194304 | tf_op jit(solution)/shard_map/all_to_all | solution.py:15
  419.8 26.8 %all-gather.5.cloned.1.call-start = ((), (), s32[]{:S(2)}) async-start(), calls=%async_computation.9 | async-start | bytes 1179648 | tf_op jit(solution)/shard_map/all_gather | solution.py:76
  420.4 162.5 %reduce-scatter.11.cloned.1.call-start = ((), (), s32[]{:S(2)}) async-start(), calls=%async_computation.11 | async-start | bytes 1179648 | tf_op jit(solution)/shard_map/reduce_scatter | solution.py:94
  468.4 2.8 copy-start.10
  471.3 3.9 copy-start.8
  495.3 3.9 copy-start.8
  519.4 3.9 copy-start.8
  540.7 2.8 copy-start.10
  543.5 3.9 copy-start.8
  555.5 105.6 %reduce-scatter.9.cloned.1.call-start = ((), (), s32[]{:S(2)}) async-start(), calls=%async_computation.10 | async-start | bytes 2228224 | tf_op jit(solution)/shard_map/reduce_scatter | solution.py:88
  555.6 105.6 %copy-start.3 = (f32[16,2048]{1,0:T(8,128)S(1)}, f32[16,2048]{1,0:T(8,128)}, u32[]{:S(2)}) copy-start(f32[16,2048]{1,0:T(8,128)} %copy-done.2) | copy-start | bytes 393220
  555.6 172.6 %copy-start.15 = (f32[16]{0:T(128)S(1)}, f32[16]{0:T(128)}, u32[]{:S(2)}) copy-start(f32[16]{0:T(128)} %copy-done.14) | copy-start | bytes 196
  555.6 172.6 %copy-start.1 = (f32[16,2048]{1,0:T(8,128)S(1)}, f32[16,2048]{1,0:T(8,128)}, u32[]{:S(2)}) copy-start(f32[16,2048]{1,0:T(8,128)} %param.8) | copy-start | bytes 393220
  555.6 172.6 %copy-start.5 = (f32[16,2048]{1,0:T(8,128)S(1)}, f32[16,2048]{1,0:T(8,128)}, u32[]{:S(2)}) copy-start(f32[16,2048]{1,0:T(8,128)} %copy-done.4) | copy-start | bytes 393220
  555.6 172.6 %copy-start.12 = (f32[16]{0:T(128)S(1)}, f32[16]{0:T(128)}, u32[]{:S(2)}) copy-start(f32[16]{0:T(128)} %copy-done.11) | copy-start | bytes 196
  (4 other events, 7.7 us)
Sparse Core Ops, SparseCore 0:
  20.6 25.6 all-gather.2
  169.8 34.0 reduce-scatter.6
  207.2 75.0 reduce-scatter.4
  422.6 23.9 all-gather.4
  555.6 27.2 reduce-scatter.10
  586.0 75.1 reduce-scatter.8
